TPU v7x, 256 devices: a whole 4x4x8 slice. The times are simulated.
256 devices in a mesh: dp: 8 (over y, core), ctx: 32 (over x, z).
Axes of the slice: x: 4, y: 4, z: 8, core: 2. Of those that a mesh axis runs over, the one named last changes fastest.
Arguments:
- queries: bfloat16 [8, 8192, 2560], P('dp', 'ctx'), may hold values from -120 to 120
- global_keys: bfloat16 [8, 8192, 512], P('dp', 'ctx'), may hold values from -5 to 5
- global_values: bfloat16 [8, 8192, 512], P('dp', 'ctx'), may hold values from -6 to 6
- out_grad: bfloat16 [8, 8192, 2560], P('dp', 'ctx'), may hold values from -6 to 6
- query_gain: float32 [2560], replicated, may hold values from 0.5 to 1.5
- doc_start: int32 [8, 64], P('dp', 'ctx'), may hold values from 0 to 63, as said below
Outputs:
- attn_out: bfloat16 [8, 8192, 2560], P('dp', 'ctx')
- query_grad: bfloat16 [8, 8192, 2560], P('dp', 'ctx')
- key_grad: bfloat16 [8, 8192, 512], P('dp', 'ctx')
- value_grad: bfloat16 [8, 8192, 512], P('dp', 'ctx')
- gain_grad: float32 [2560], replicated
Inputs may be any that keep to these rules, and one draw needn't show every extreme that they name: doc_start[g, b] is the first block of block b's document: it is at most b and at least b - 6, never falls along b, and equals b where a document begins; every slab has a document of exactly 7 blocks.
All inputs are finite; a program needn't handle non-finite values.
Results may differ from a plain program's by a relative error of at most 0.017.
The roundings to bfloat16 on the way count: a program that leaves them out, or rounds other values in their place, can miss the bound.
Values may be sent and summed in bfloat16 or wider, within the bound.
No kernel may reach another device: no remote copies, remote signals or barrier semaphores. Data moves between devices by JAX's collectives and lax.ppermute only.
A program may use at most 64 MiB of HBM per device.

v0:
```python
import math
import jax
import jax.numpy as jnp
from jax import lax
from jax.sharding import PartitionSpec as P

HD = 128
BLOCK = 128
REACH = 4


def shifted(value, axis, steps):
    count = lax.axis_size(axis)
    first, last = (max(0, -steps), min(count, count - steps))
    return lax.ppermute(value, axis, [(source, source + steps) for source in range(first, last)])


def head_group(inputs, allowed, factor):
    query_part, key_part, value_part, grad_part = inputs
    scores = (
        jnp.einsum("tgd,wd->gtw", query_part, key_part, preferred_element_type=jnp.float32) * factor
    )
    scores = jnp.where(allowed[None], scores, -jnp.inf)
    row_max = jnp.max(scores, axis=-1, keepdims=True)
    log_total = row_max + jnp.log(jnp.sum(jnp.exp(scores - row_max), axis=-1, keepdims=True))
    weights = jnp.exp(scores - log_total)
    weights_low = weights.astype(jnp.bfloat16)
    result = jnp.einsum(
        "gtw,wd->tgd", weights_low, value_part, preferred_element_type=jnp.float32
    ).astype(jnp.bfloat16)
    inner_sum = jnp.einsum("tgd,tgd->gt", grad_part, result, preferred_element_type=jnp.float32)
    dweights = jnp.einsum("tgd,wd->gtw", grad_part, value_part, preferred_element_type=jnp.float32)
    dscore_low = (weights * (dweights - inner_sum[..., None])).astype(jnp.bfloat16)
    dquery = (
        jnp.einsum("gtw,wd->tgd", dscore_low, key_part, preferred_element_type=jnp.float32) * factor
    )
    dkey = (
        jnp.einsum("gtw,tgd->wd", dscore_low, query_part, preferred_element_type=jnp.float32)
        * factor
    )
    dvalue = jnp.einsum("gtw,tgd->wd", weights_low, grad_part, preferred_element_type=jnp.float32)
    return (result, dquery, dkey, dvalue)


def local(queries, global_keys, global_values, out_grad, query_gain, doc_start):
    row_count = queries.shape[1]
    reach = REACH
    width = reach * row_count
    device = lax.axis_index("ctx")
    query_rows = queries[0]
    key_rows = global_keys[0]
    value_rows = global_values[0]
    grad_rows = out_grad[0]
    kv_count = key_rows.shape[1] // HD
    group_size = query_rows.shape[1] // (kv_count * HD)
    factor = 1.0 / math.sqrt(HD)
    scaled = (query_rows.astype(jnp.float32) * query_gain).astype(jnp.bfloat16)
    key_list = [key_rows]
    value_list = [value_rows]
    for distance in range(1, reach):
        far_keys, far_values = shifted((key_rows, value_rows), "ctx", distance)
        key_list.insert(0, far_keys)
        value_list.insert(0, far_values)
    window_keys = jnp.concatenate(key_list, axis=0)
    window_values = jnp.concatenate(value_list, axis=0)
    first_device = device - (reach - 1)
    query_pos = device * row_count + jnp.arange(row_count, dtype=jnp.int32)
    key_pos = first_device * row_count + jnp.arange(width, dtype=jnp.int32)
    begins = jnp.repeat(doc_start[0], BLOCK) * BLOCK
    allowed = (key_pos[None, :] <= query_pos[:, None]) & (key_pos[None, :] >= begins[:, None])
    query_four = scaled.reshape(row_count, kv_count, group_size, HD).transpose(1, 0, 2, 3)
    grad_four = grad_rows.reshape(row_count, kv_count, group_size, HD).transpose(1, 0, 2, 3)
    key_three = window_keys.reshape(width, kv_count, HD).transpose(1, 0, 2)
    value_three = window_values.reshape(width, kv_count, HD).transpose(1, 0, 2)
    results, dqueries, dkeys, dvalues = lax.map(
        lambda inputs: head_group(inputs, allowed, factor),
        (query_four, key_three, value_three, grad_four),
    )
    attn_out = results.transpose(1, 0, 2, 3).reshape(row_count, -1)
    dscaled = dqueries.transpose(1, 0, 2, 3).reshape(row_count, -1)

    def by_offset(partial_value):
        return partial_value.reshape(kv_count, reach, row_count, HD)[:, ::-1]

    key_offsets = by_offset(dkeys)
    value_offsets = by_offset(dvalues)
    key_total = key_offsets[:, 0]
    value_total = value_offsets[:, 0]
    for distance in range(1, reach):
        got_keys, got_values = shifted(
            (key_offsets[:, distance], value_offsets[:, distance]), "ctx", -distance
        )
        key_total = key_total + got_keys
        value_total = value_total + got_values
    key_grad = key_total.transpose(1, 0, 2).reshape(row_count, -1).astype(jnp.bfloat16)
    value_grad = value_total.transpose(1, 0, 2).reshape(row_count, -1).astype(jnp.bfloat16)
    query_grad = (dscaled * query_gain).astype(jnp.bfloat16)
    gain_term = jnp.sum(dscaled * query_rows.astype(jnp.float32), axis=0)
    gain_grad = lax.psum(gain_term, ("dp", "ctx"))
    return (attn_out[None], query_grad[None], key_grad[None], value_grad[None], gain_grad)


def solution(mesh):
    return jax.shard_map(
        local,
        mesh=mesh,
        in_specs=(
            P("dp", "ctx", None),
            P("dp", "ctx", None),
            P("dp", "ctx", None),
            P("dp", "ctx", None),
            P(),
            P("dp", "ctx"),
        ),
        out_specs=(
            P("dp", "ctx", None),
            P("dp", "ctx", None),
            P("dp", "ctx", None),
            P("dp", "ctx", None),
            P(),
        ),
        check_vma=False,
    )
```

profile of v0, /device:TPU:1, one launch (start us, length us, event | category | flops | bytes accessed | tf_op | source)
XLA Modules:
  0.0 343.3 jit_solution(1276972712751430127)
XLA Ops:
  1.7 5.1 %collective-permute-start.5 = (bf16[256,512]{0,1:T(8,128)(2,1)S(1)}, bf16[256,512]{0,1:T(8,128)(2,1)}, u32[]{:S(2)}, u32[]{:S(2)}) collective-permute-start(bf16[256,512]{0,1:T(8,128)(2,1)S(1)} %bitcast.227), channel_id=1, source_target_pairs={{0,1},{1,2},{2,3},{3,4},{4,5},{5,6},{6,7},{7,8},{8,9},{9,10},{10,1... | collective-permute-start | bytes 786440 | tf_op jit(solution)/shard_map/ppermute | solution.py:15
  6.8 4.9 %collective-permute-start.4 = (bf16[256,512]{0,1:T(8,128)(2,1)S(1)}, bf16[256,512]{0,1:T(8,128)(2,1)}, u32[]{:S(2)}, u32[]{:S(2)}) collective-permute-start(bf16[256,512]{0,1:T(8,128)(2,1)S(1)} %bitcast.228), channel_id=1, source_target_pairs={{0,2},{1,3},{2,4},{3,5},{4,6},{5,7},{6,8},{7,9},{8,10},{9,11},{10,... | collective-permute-start | bytes 786440 | tf_op jit(solution)/shard_map/ppermute | solution.py:15
  11.7 5.7 %collective-permute-start.3 = (bf16[256,512]{0,1:T(8,128)(2,1)S(1)}, bf16[256,512]{0,1:T(8,128)(2,1)}, u32[]{:S(2)}, u32[]{:S(2)}) collective-permute-start(bf16[256,512]{0,1:T(8,128)(2,1)S(1)} %bitcast.229), channel_id=1, source_target_pairs={{0,3},{1,4},{2,5},{3,6},{4,7},{5,8},{6,9},{7,10},{8,11},{9,12},{10... | collective-permute-start | bytes 786440 | tf_op jit(solution)/shard_map/ppermute | solution.py:15
  17.4 2.6 collective-permute-start.2
  20.0 2.3 collective-permute-start.1
  26.5 17.9 %collective-permute-done.2 = bf16[256,512]{1,0:T(8,128)(2,1)S(1)} collective-permute-done((bf16[256,512]{1,0:T(8,128)(2,1)}, bf16[256,512]{1,0:T(8,128)(2,1)S(1)}, u32[]{:S(2)}, u32[]{:S(2)}) %collective-permute-start.2) | collective-permute-done | bytes 262176 | tf_op jit(solution)/shard_map/ppermute | solution.py:15
  44.5 9.5 %collective-permute-start = (bf16[256,512]{1,0:T(8,128)(2,1)S(1)}, bf16[256,512]{1,0:T(8,128)(2,1)}, u32[]{:S(2)}, u32[]{:S(2)}) collective-permute-start(bf16[256,512]{1,0:T(8,128)(2,1)S(1)} %bitcast.240), channel_id=1, source_target_pairs={{0,3},{1,4},{2,5},{3,6},{4,7},{5,8},{6,9},{7,10},{8,11},{9,12},{10... | collective-permute-start | bytes 786440 | tf_op jit(solution)/shard_map/ppermute | solution.py:15
  54.1 2.5 copy.42
  63.4 68.0 %while.17 = (s32[]{:T(128)}, bf16[4,256,5,128]{1,3,2,0:T(8,128)(2,1)}, f32[4,256,5,128]{1,3,2,0:T(8,128)}, f32[4,1024,128]{2,1,0:T(8,128)}, f32[4,1024,128]{2,1,...) while((s32[]{:T(128)}, ...), condition=%wide.region_3.4_spmd.clone, body=%wide.region_0.3_spmd.clone.sunk | while | flops 2042689024 | bytes 49229988 | solution.py:75
  70.7 3.1 fusion.75
  73.8 2.6 fusion.72
  78.1 2.3 fusion.73
  87.7 3.1 fusion.75
  90.8 2.6 fusion.72
  95.1 2.3 fusion.73
  104.7 3.1 fusion.75
  107.8 2.6 fusion.72
  112.1 2.3 fusion.73
  121.7 3.1 fusion.75
  124.8 2.6 fusion.72
  129.1 2.3 fusion.73
  145.0 33.2 %collective-permute-done.11 = f32[4,256,128]{2,0,1:T(4,128)S(1)} collective-permute-done((f32[4,256,128]{2,0,1:T(4,128)S(1)}, f32[4,256,128]{2,0,1:T(4,128)S(1)}, u32[]{:S(2)}, u32[]{:S(2)}) %collective-permute-start.11) | collective-permute-done | bytes 524320 | tf_op jit(solution)/shard_map/ppermute | solution.py:15
  180.0 2.4 copy.54
  184.0 153.9 %psum.7 = f32[2560]{0:T(1024)} all-reduce(f32[2560]{0:T(1024)S(1)} %reduce_sum.21), channel_id=1, replica_groups=mesh['dp'=8,'ctx'=32] {'dp','ctx'}, use_global_device_ids=true, to_apply=%region_5.6 | all-reduce | flops 2560 | bytes 20480 | tf_op jit(solution)/shard_map/psum | solution.py:99
  (122 shorter events, 69.8 us)
Async XLA Ops:
  1.7 57.2 %collective-permute-start.5 = (bf16[256,512]{0,1:T(8,128)(2,1)S(1)}, bf16[256,512]{0,1:T(8,128)(2,1)}, u32[]{:S(2)}, u32[]{:S(2)}) collective-permute-start(bf16[256,512]{0,1:T(8,128)(2,1)S(1)} %bitcast.227), channel_id=1, source_target_pairs={{0,1},{1,2},{2,3},{3,4},{4,5},{5,6},{6,7},{7,8},{8,9},{9,10},{10,1... | collective-permute-start | bytes 786440 | tf_op jit(solution)/shard_map/ppermute | solution.py:15
  6.8 52.1 %collective-permute-start.4 = (bf16[256,512]{0,1:T(8,128)(2,1)S(1)}, bf16[256,512]{0,1:T(8,128)(2,1)}, u32[]{:S(2)}, u32[]{:S(2)}) collective-permute-start(bf16[256,512]{0,1:T(8,128)(2,1)S(1)} %bitcast.228), channel_id=1, source_target_pairs={{0,2},{1,3},{2,4},{3,5},{4,6},{5,7},{6,8},{7,9},{8,10},{9,11},{10,... | collective-permute-start | bytes 786440 | tf_op jit(solution)/shard_map/ppermute | solution.py:15
  11.7 47.2 %collective-permute-start.3 = (bf16[256,512]{0,1:T(8,128)(2,1)S(1)}, bf16[256,512]{0,1:T(8,128)(2,1)}, u32[]{:S(2)}, u32[]{:S(2)}) collective-permute-start(bf16[256,512]{0,1:T(8,128)(2,1)S(1)} %bitcast.229), channel_id=1, source_target_pairs={{0,3},{1,4},{2,5},{3,6},{4,7},{5,8},{6,9},{7,10},{8,11},{9,12},{10... | collective-permute-start | bytes 786440 | tf_op jit(solution)/shard_map/ppermute | solution.py:15
  17.4 27.1 %collective-permute-start.2 = (bf16[256,512]{1,0:T(8,128)(2,1)}, bf16[256,512]{1,0:T(8,128)(2,1)S(1)}, u32[]{:S(2)}, u32[]{:S(2)}) collective-permute-start(bf16[256,512]{1,0:T(8,128)(2,1)} %bitcast.238), channel_id=1, source_target_pairs={{0,1},{1,2},{2,3},{3,4},{4,5},{5,6},{6,7},{7,8},{8,9},{9,10},{10,1... | collective-permute-start | bytes 786440 | tf_op jit(solution)/shard_map/ppermute | solution.py:15
  20.0 37.7 %collective-permute-start.1 = (bf16[256,512]{1,0:T(8,128)(2,1)}, bf16[256,512]{1,0:T(8,128)(2,1)}, u32[]{:S(2)}, u32[]{:S(2)}) collective-permute-start(bf16[256,512]{1,0:T(8,128)(2,1)} %bitcast.239), channel_id=1, source_target_pairs={{0,2},{1,3},{2,4},{3,5},{4,6},{5,7},{6,8},{7,9},{8,10},{9,11},{10,... | collective-permute-start | bytes 786440 | tf_op jit(solution)/shard_map/ppermute | solution.py:15
  24.7 31.9 %copy-start = (f32[1,256,2560]{1,2,0:T(8,128)}, f32[1,256,2560]{1,2,0:T(8,128)S(1)}, u32[]{:S(2)}) copy-start(f32[1,256,2560]{1,2,0:T(8,128)S(1)} %copy.41) | copy-start | bytes 7864324
  24.7 1.8 copy-start.10
  24.7 19.7 %copy-start.7 = (bf16[1,256,512]{2,1,0:T(8,128)(2,1)S(1)}, bf16[1,256,512]{2,1,0:T(8,128)(2,1)}, u32[]{:S(2)}) copy-start(bf16[1,256,512]{2,1,0:T(8,128)(2,1)} %param.10) | copy-start | bytes 786436
  44.5 9.5 %copy-start.8 = (bf16[256,512]{1,0:T(8,128)(2,1)}, bf16[256,512]{1,0:T(8,128)(2,1)S(1)}, u32[]{:S(2)}) copy-start(bf16[256,512]{1,0:T(8,128)(2,1)S(1)} %collective-permute-done.2) | copy-start | bytes 786436
  44.5 16.7 %collective-permute-start = (bf16[256,512]{1,0:T(8,128)(2,1)S(1)}, bf16[256,512]{1,0:T(8,128)(2,1)}, u32[]{:S(2)}, u32[]{:S(2)}) collective-permute-start(bf16[256,512]{1,0:T(8,128)(2,1)S(1)} %bitcast.240), channel_id=1, source_target_pairs={{0,3},{1,4},{2,5},{3,6},{4,7},{5,8},{6,9},{7,10},{8,11},{9,12},{10... | collective-permute-start | bytes 786440 | tf_op jit(solution)/shard_map/ppermute | solution.py:15
  57.7 5.7 %copy-start.2 = (bf16[4,256,5,128]{1,3,2,0:T(8,128)(2,1)S(1)}, bf16[4,256,5,128]{1,3,2,0:T(8,128)(2,1)}, u32[]{:S(2)}) copy-start(bf16[4,256,5,128]{1,3,2,0:T(8,128)(2,1)} %fusion.35) | copy-start | bytes 3932164
  67.1 1.2 copy-start.5
  101.1 1.2 copy-start.5
  133.1 6.1 %copy-start.3 = (f32[4,256,5,128]{1,3,2,0:T(8,128)S(1)}, f32[4,256,5,128]{1,3,2,0:T(8,128)}, u32[]{:S(2)}) copy-start(f32[4,256,5,128]{1,3,2,0:T(8,128)} %get-tuple-element.61) | copy-start | bytes 7864324
  133.1 6.1 %copy-start.9 = (f32[2560]{0:T(1024)S(1)}, f32[2560]{0:T(1024)}, u32[]{:S(2)}) copy-start(f32[2560]{0:T(1024)} %param.12) | copy-start | bytes 30724
  134.6 5.0 %copy-start.4 = (f32[4,1024,128]{2,1,0:T(8,128)S(1)}, f32[4,1024,128]{2,1,0:T(8,128)}, u32[]{:S(2)}) copy-start(f32[4,1024,128]{2,1,0:T(8,128)} %get-tuple-element.62) | copy-start | bytes 6291460
  134.9 43.2 %collective-permute-start.11 = (f32[4,256,128]{2,0,1:T(4,128)S(1)}, f32[4,256,128]{2,0,1:T(4,128)S(1)}, u32[]{:S(2)}, u32[]{:S(2)}) collective-permute-start(f32[4,256,128]{2,0,1:T(4,128)S(1)} %bitcast.237), channel_id=1, source_target_pairs={{3,0},{4,1},{5,2},{6,3},{7,4},{8,5},{9,6},{10,7},{11,8},{12,9},{13... | collective-permute-start | bytes 1572872 | tf_op jit(solution)/shard_map/ppermute | solution.py:15
  136.4 201.5 %collective-permute-start.9 = (f32[4,256,128]{2,0,1:T(4,128)}, f32[4,256,128]{2,0,1:T(4,128)}, u32[]{:S(2)}, u32[]{:S(2)}) collective-permute-start(f32[4,256,128]{2,0,1:T(4,128)} %bitcast.170), channel_id=1, source_target_pairs={{1,0},{2,1},{3,2},{4,3},{5,4},{6,5},{7,6},{8,7},{9,8},{10,9},{11,1... | collective-permute-start | bytes 1572872 | tf_op jit(solution)/shard_map/ppermute | solution.py:15
  137.7 200.2 %collective-permute-start.10 = (f32[4,256,128]{2,0,1:T(4,128)S(1)}, f32[4,256,128]{2,0,1:T(4,128)}, u32[]{:S(2)}, u32[]{:S(2)}) collective-permute-start(f32[4,256,128]{2,0,1:T(4,128)S(1)} %bitcast.235), channel_id=1, source_target_pairs={{2,0},{3,1},{4,2},{5,3},{6,4},{7,5},{8,6},{9,7},{10,8},{11,9},{12,... | collective-permute-start | bytes 1572872 | tf_op jit(solution)/shard_map/ppermute | solution.py:15
  139.8 39.7 %copy-start.1 = (f32[1,256,2560]{1,2,0:T(8,128)S(1)}, f32[1,256,2560]{1,2,0:T(8,128)}, u32[]{:S(2)}) copy-start(f32[1,256,2560]{1,2,0:T(8,128)} %copy-done) | copy-start | bytes 7864324
  142.4 198.2 %collective-permute-start.8 = (f32[4,256,128]{2,0,1:T(4,128)}, f32[4,256,128]{2,0,1:T(4,128)}, u32[]{:S(2)}, u32[]{:S(2)}) collective-permute-start(f32[4,256,128]{2,0,1:T(4,128)} %bitcast.171), channel_id=1, source_target_pairs={{3,0},{4,1},{5,2},{6,3},{7,4},{8,5},{9,6},{10,7},{11,8},{12,9},{13... | collective-permute-start | bytes 1572872 | tf_op jit(solution)/shard_map/ppermute | solution.py:15
  143.7 196.9 %collective-permute-start.6 = (f32[4,256,128]{2,0,1:T(4,128)}, f32[4,256,128]{2,0,1:T(4,128)}, u32[]{:S(2)}, u32[]{:S(2)}) collective-permute-start(f32[4,256,128]{2,0,1:T(4,128)} %bitcast.173), channel_id=1, source_target_pairs={{1,0},{2,1},{3,2},{4,3},{5,4},{6,5},{7,6},{8,7},{9,8},{10,9},{11,1... | collective-permute-start | bytes 1572872 | tf_op jit(solution)/shard_map/ppermute | solution.py:15
  178.2 1.3 copy-start.6
  178.2 162.4 %collective-permute-start.7 = (f32[4,256,128]{2,0,1:T(4,128)S(1)}, f32[4,256,128]{2,0,1:T(4,128)}, u32[]{:S(2)}, u32[]{:S(2)}) collective-permute-start(f32[4,256,128]{2,0,1:T(4,128)S(1)} %bitcast.236), channel_id=1, source_target_pairs={{2,0},{3,1},{4,2},{5,3},{6,4},{7,5},{8,6},{9,7},{10,8},{11,9},{12,... | collective-permute-start | bytes 1572872 | tf_op jit(solution)/shard_map/ppermute | solution.py:15
  (2 other events, 2.5 us)
where the time goes:
time: 345 us; the launch traced here: 343 us
  blocking collectives  154 us (45%)
  matrix products  55.5 us (16%)
  waiting for transfers between devices  51.1 us (15%)
  starting transfers between devices  38.2 us (11%)
  local copies, waits for them, and re-layouts  27.5 us (8%)
  other arithmetic  15.8 us (5%)
    psum x1, blocking collectives, local(): gain_grad = lax.psum(gain_term, ('dp', 'ctx'))  154 us
    ppermute x12, waiting for transfers between devices, shifted(): lax.ppermute(value, axis, [(source, source + steps) for source in range(f...  51.1 us
    ppermute x12, starting transfers between devices, shifted(): lax.ppermute(value, axis, [(source, source + steps) for source in range(f...  38.2 us
    dot_general x4, matrix products, head_group(): jnp.einsum('gtw,tgd->wd', weights_low, grad_part, preferred_element_type=...  12.5 us
    unnamed x31, local copies, waits for them, and re-layouts  12.2 us
    dot_general x4, matrix products, head_group(): jnp.einsum('tgd,wd->gtw', grad_part, value_part, preferred_element_type=j...  10.4 us
    dot_general x4, matrix products, head_group(): jnp.einsum('gtw,wd->tgd', dscore_low, key_part, preferred_element_type=jn...  9.25 us
    dot_general x4, matrix products, head_group(): jnp.einsum('gtw,wd->tgd', weights_low, value_part, preferred_element_type...  8.8 us
  transfers between devices with their start and end apart: 12, of which 2 were waited for; matrix products, arithmetic and copies ran while one was open for 6% of the time, Pallas kernels for 0%

commit v1 on v0

--- a/solution.py
+++ b/solution.py
@@ -96,7 +96,7 @@
     value_grad = value_total.transpose(1, 0, 2).reshape(row_count, -1).astype(jnp.bfloat16)
     query_grad = (dscaled * query_gain).astype(jnp.bfloat16)
     gain_term = jnp.sum(dscaled * query_rows.astype(jnp.float32), axis=0)
-    gain_grad = lax.psum(gain_term, ("dp", "ctx"))
+    gain_grad = jnp.sum(lax.all_gather(gain_term, ("dp", "ctx")), axis=0)
     return (attn_out[None], query_grad[None], key_grad[None], value_grad[None], gain_grad)
 
 

time: 345 us -> 333 us (0.965)
  the two profiles are of different devices: /device:TPU:1 before, /device:TPU:51 now
where the time goes in v1:
time: 333 us; the launch traced here: 332 us
  waiting for transfers between devices  167 us (50%)
  matrix products  55.5 us (17%)
  starting transfers between devices  44.5 us (13%)
  local copies, waits for them, and re-layouts  27.4 us (8%)
  other arithmetic  22.3 us (7%)
  between operations  14.4 us (4%)
    ppermute x12, waiting for transfers between devices, shifted(): lax.ppermute(value, axis, [(source, source + steps) for source in range(f...  135 us
    ppermute x12, starting transfers between devices, shifted(): lax.ppermute(value, axis, [(source, source + steps) for source in range(f...  44.4 us
    all_gather x1, waiting for transfers between devices, local(): gain_grad = jnp.sum(lax.all_gather(gain_term, ('dp', 'ctx')), axis=0)  32 us
    unnamed x32, local copies, waits for them, and re-layouts  13.6 us
    dot_general x4, matrix products, head_group(): jnp.einsum('gtw,tgd->wd', weights_low, grad_part, preferred_element_type=...  12.5 us
    dot_general x4, matrix products, head_group(): jnp.einsum('tgd,wd->gtw', grad_part, value_part, preferred_element_type=j...  10.4 us
    dot_general x4, matrix products, head_group(): jnp.einsum('gtw,wd->tgd', dscore_low, key_part, preferred_element_type=jn...  9.26 us
    dot_general x4, matrix products, head_group(): jnp.einsum('gtw,wd->tgd', weights_low, value_part, preferred_element_type...  8.8 us
  transfers between devices with their start and end apart: 13, of which 9 were waited for; matrix products, arithmetic and copies ran while one was open for 8% of the time, Pallas kernels for 0%

profile of v1, /device:TPU:51, one launch (start us, length us, event | category | flops | bytes accessed | tf_op | source)
XLA Modules:
  0.0 331.5 jit_solution(278309342295783716)
XLA Ops:
  8.3 3.5 %collective-permute-start.5 = (bf16[256,512]{0,1:T(8,128)(2,1)S(1)}, bf16[256,512]{0,1:T(8,128)(2,1)}, u32[]{:S(2)}, u32[]{:S(2)}) collective-permute-start(bf16[256,512]{0,1:T(8,128)(2,1)S(1)} %bitcast.227), channel_id=1, source_target_pairs={{0,1},{1,2},{2,3},{3,4},{4,5},{5,6},{6,7},{7,8},{8,9},{9,10},{10,1... | collective-permute-start | bytes 786440 | tf_op jit(solution)/shard_map/ppermute | solution.py:15
  11.9 6.1 %collective-permute-start.4 = (bf16[256,512]{0,1:T(8,128)(2,1)S(1)}, bf16[256,512]{0,1:T(8,128)(2,1)}, u32[]{:S(2)}, u32[]{:S(2)}) collective-permute-start(bf16[256,512]{0,1:T(8,128)(2,1)S(1)} %bitcast.228), channel_id=1, source_target_pairs={{0,2},{1,3},{2,4},{3,5},{4,6},{5,7},{6,8},{7,9},{8,10},{9,11},{10,... | collective-permute-start | bytes 786440 | tf_op jit(solution)/shard_map/ppermute | solution.py:15
  18.0 3.6 %collective-permute-start.3 = (bf16[256,512]{0,1:T(8,128)(2,1)S(1)}, bf16[256,512]{0,1:T(8,128)(2,1)}, u32[]{:S(2)}, u32[]{:S(2)}) collective-permute-start(bf16[256,512]{0,1:T(8,128)(2,1)S(1)} %bitcast.229), channel_id=1, source_target_pairs={{0,3},{1,4},{2,5},{3,6},{4,7},{5,8},{6,9},{7,10},{8,11},{9,12},{10... | collective-permute-start | bytes 786440 | tf_op jit(solution)/shard_map/ppermute | solution.py:15
  23.5 2.9 collective-permute-start.1
  30.5 21.2 %collective-permute-done.2 = bf16[256,512]{1,0:T(8,128)(2,1)S(1)} collective-permute-done((bf16[256,512]{1,0:T(8,128)(2,1)}, bf16[256,512]{1,0:T(8,128)(2,1)S(1)}, u32[]{:S(2)}, u32[]{:S(2)}) %collective-permute-start.2) | collective-permute-done | bytes 262176 | tf_op jit(solution)/shard_map/ppermute | solution.py:15
  51.7 11.5 %collective-permute-start = (bf16[256,512]{1,0:T(8,128)(2,1)S(1)}, bf16[256,512]{1,0:T(8,128)(2,1)}, u32[]{:S(2)}, u32[]{:S(2)}) collective-permute-start(bf16[256,512]{1,0:T(8,128)(2,1)S(1)} %bitcast.239), channel_id=1, source_target_pairs={{0,3},{1,4},{2,5},{3,6},{4,7},{5,8},{6,9},{7,10},{8,11},{9,12},{10... | collective-permute-start | bytes 786440 | tf_op jit(solution)/shard_map/ppermute | solution.py:15
  70.5 13.6 %collective-permute-done = bf16[256,512]{1,0:T(8,128)(2,1)} collective-permute-done((bf16[256,512]{1,0:T(8,128)(2,1)S(1)}, bf16[256,512]{1,0:T(8,128)(2,1)}, u32[]{:S(2)}, u32[]{:S(2)}) %collective-permute-start) | collective-permute-done | bytes 262176 | tf_op jit(solution)/shard_map/ppermute | solution.py:15
  86.3 68.1 %while.17 = (s32[]{:T(128)}, bf16[4,256,5,128]{1,3,2,0:T(8,128)(2,1)}, f32[4,256,5,128]{1,3,2,0:T(8,128)}, f32[4,1024,128]{2,1,0:T(8,128)}, f32[4,1024,128]{2,1,...) while((s32[]{:T(128)}, ...), condition=%wide.region_3.4_spmd.clone, body=%wide.region_0.3_spmd.clone.sunk | while | flops 2042689024 | bytes 49229988 | solution.py:75
  93.6 3.1 fusion.75
  110.6 3.2 fusion.75
  113.8 2.6 fusion.72
  127.7 3.1 fusion.75
  130.8 2.6 fusion.72
  144.7 3.1 fusion.75
  154.4 3.1 fusion.34
  158.7 5.0 %collective-permute-start.11 = (f32[4,256,128]{2,0,1:T(4,128)S(1)}, f32[4,256,128]{2,0,1:T(4,128)S(1)}, u32[]{:S(2)}, u32[]{:S(2)}) collective-permute-start(f32[4,256,128]{2,0,1:T(4,128)S(1)} %bitcast.236), channel_id=1, source_target_pairs={{3,0},{4,1},{5,2},{6,3},{7,4},{8,5},{9,6},{10,7},{11,8},{12,9},{13... | collective-permute-start | bytes 1572872 | tf_op jit(solution)/shard_map/ppermute | solution.py:15
  176.9 21.6 %collective-permute-done.11 = f32[4,256,128]{2,0,1:T(4,128)S(1)} collective-permute-done((f32[4,256,128]{2,0,1:T(4,128)S(1)}, f32[4,256,128]{2,0,1:T(4,128)S(1)}, u32[]{:S(2)}, u32[]{:S(2)}) %collective-permute-start.11) | collective-permute-done | bytes 524320 | tf_op jit(solution)/shard_map/ppermute | solution.py:15
  204.8 5.1 %collective-permute-done.9 = f32[4,256,128]{2,0,1:T(4,128)} collective-permute-done((f32[4,256,128]{2,0,1:T(4,128)}, f32[4,256,128]{2,0,1:T(4,128)}, u32[]{:S(2)}, u32[]{:S(2)}) %collective-permute-start.9) | collective-permute-done | bytes 524320 | tf_op jit(solution)/shard_map/ppermute | solution.py:15
  209.9 9.2 %collective-permute-done.10 = f32[4,256,128]{2,0,1:T(4,128)} collective-permute-done((f32[4,256,128]{2,0,1:T(4,128)}, f32[4,256,128]{2,0,1:T(4,128)}, u32[]{:S(2)}, u32[]{:S(2)}) %collective-permute-start.10) | collective-permute-done | bytes 524320 | tf_op jit(solution)/shard_map/ppermute | solution.py:15
  221.7 45.2 %collective-permute-done.8 = f32[4,256,128]{2,0,1:T(4,128)} collective-permute-done((f32[4,256,128]{2,0,1:T(4,128)}, f32[4,256,128]{2,0,1:T(4,128)}, u32[]{:S(2)}, u32[]{:S(2)}) %collective-permute-start.8) | collective-permute-done | bytes 524320 | tf_op jit(solution)/shard_map/ppermute | solution.py:15
  266.9 11.3 %collective-permute-done.6 = f32[4,256,128]{2,0,1:T(4,128)} collective-permute-done((f32[4,256,128]{2,0,1:T(4,128)}, f32[4,256,128]{2,0,1:T(4,128)}, u32[]{:S(2)}, u32[]{:S(2)}) %collective-permute-start.6) | collective-permute-done | bytes 524320 | tf_op jit(solution)/shard_map/ppermute | solution.py:15
  278.2 8.0 %collective-permute-done.7 = f32[4,256,128]{2,0,1:T(4,128)} collective-permute-done((f32[4,256,128]{2,0,1:T(4,128)S(1)}, f32[4,256,128]{2,0,1:T(4,128)}, u32[]{:S(2)}, u32[]{:S(2)}) %collective-permute-start.7) | collective-permute-done | bytes 524320 | tf_op jit(solution)/shard_map/ppermute | solution.py:15
  288.9 32.0 %all-gather.3.cloned.1.call-done = f32[256,1,2560]{2,1,0:T(1,128)} async-done(((f32[1,1,2560]{2,1,0:T(1,128)}), f32[256,1,2560]{2,1,0:T(1,128)}) %all-gather.3.cloned.1.call-update) | async-done | bytes 2621456 | tf_op jit(solution)/shard_map/all_gather | solution.py:99
  320.9 3.8 %reduce_sum.28 = f32[2560]{0:T(1024)} reduce(f32[256,1,2560]{2,1,0:T(1,128)} %all-gather.3.cloned.1.call-done, f32[]{:T(128)} %constant.11.clone.1), dimensions={0,1}, to_apply=%region_5.6 | reduce | flops 652800 | bytes 2631684 | tf_op jit(solution)/shard_map/reduce_sum | solution.py:99
  (125 shorter events, 92.4 us)
Async XLA Ops:
  7.2 313.7 %all-gather.3.cloned.1.call-start = ((), (), s32[]{:S(2)}) async-start(), calls=%async_computation | async-start | bytes 2631680 | tf_op jit(solution)/shard_map/all_gather | solution.py:99
  8.3 59.9 %collective-permute-start.5 = (bf16[256,512]{0,1:T(8,128)(2,1)S(1)}, bf16[256,512]{0,1:T(8,128)(2,1)}, u32[]{:S(2)}, u32[]{:S(2)}) collective-permute-start(bf16[256,512]{0,1:T(8,128)(2,1)S(1)} %bitcast.227), channel_id=1, source_target_pairs={{0,1},{1,2},{2,3},{3,4},{4,5},{5,6},{6,7},{7,8},{8,9},{9,10},{10,1... | collective-permute-start | bytes 786440 | tf_op jit(solution)/shard_map/ppermute | solution.py:15
  11.9 56.3 %collective-permute-start.4 = (bf16[256,512]{0,1:T(8,128)(2,1)S(1)}, bf16[256,512]{0,1:T(8,128)(2,1)}, u32[]{:S(2)}, u32[]{:S(2)}) collective-permute-start(bf16[256,512]{0,1:T(8,128)(2,1)S(1)} %bitcast.228), channel_id=1, source_target_pairs={{0,2},{1,3},{2,4},{3,5},{4,6},{5,7},{6,8},{7,9},{8,10},{9,11},{10,... | collective-permute-start | bytes 786440 | tf_op jit(solution)/shard_map/ppermute | solution.py:15
  18.0 50.2 %collective-permute-start.3 = (bf16[256,512]{0,1:T(8,128)(2,1)S(1)}, bf16[256,512]{0,1:T(8,128)(2,1)}, u32[]{:S(2)}, u32[]{:S(2)}) collective-permute-start(bf16[256,512]{0,1:T(8,128)(2,1)S(1)} %bitcast.229), channel_id=1, source_target_pairs={{0,3},{1,4},{2,5},{3,6},{4,7},{5,8},{6,9},{7,10},{8,11},{9,12},{10... | collective-permute-start | bytes 786440 | tf_op jit(solution)/shard_map/ppermute | solution.py:15
  21.5 30.2 %collective-permute-start.2 = (bf16[256,512]{1,0:T(8,128)(2,1)}, bf16[256,512]{1,0:T(8,128)(2,1)S(1)}, u32[]{:S(2)}, u32[]{:S(2)}) collective-permute-start(bf16[256,512]{1,0:T(8,128)(2,1)} %bitcast.237), channel_id=1, source_target_pairs={{0,1},{1,2},{2,3},{3,4},{4,5},{5,6},{6,7},{7,8},{8,9},{9,10},{10,1... | collective-permute-start | bytes 786440 | tf_op jit(solution)/shard_map/ppermute | solution.py:15
  23.5 43.5 %collective-permute-start.1 = (bf16[256,512]{1,0:T(8,128)(2,1)}, bf16[256,512]{1,0:T(8,128)(2,1)}, u32[]{:S(2)}, u32[]{:S(2)}) collective-permute-start(bf16[256,512]{1,0:T(8,128)(2,1)} %bitcast.238), channel_id=1, source_target_pairs={{0,2},{1,3},{2,4},{3,5},{4,6},{5,7},{6,8},{7,9},{8,10},{9,11},{10,... | collective-permute-start | bytes 786440 | tf_op jit(solution)/shard_map/ppermute | solution.py:15
  28.7 37.2 %copy-start = (f32[1,256,2560]{1,2,0:T(8,128)}, f32[1,256,2560]{1,2,0:T(8,128)S(1)}, u32[]{:S(2)}) copy-start(f32[1,256,2560]{1,2,0:T(8,128)S(1)} %copy.66) | copy-start | bytes 7864324
  28.7 1.8 copy-start.10
  28.7 23.0 %copy-start.7 = (bf16[1,256,512]{2,1,0:T(8,128)(2,1)S(1)}, bf16[1,256,512]{2,1,0:T(8,128)(2,1)}, u32[]{:S(2)}) copy-start(bf16[1,256,512]{2,1,0:T(8,128)(2,1)} %param.10) | copy-start | bytes 786436
  51.7 11.5 %copy-start.8 = (bf16[256,512]{1,0:T(8,128)(2,1)}, bf16[256,512]{1,0:T(8,128)(2,1)S(1)}, u32[]{:S(2)}) copy-start(bf16[256,512]{1,0:T(8,128)(2,1)S(1)} %collective-permute-done.2) | copy-start | bytes 786436
  51.7 32.4 %collective-permute-start = (bf16[256,512]{1,0:T(8,128)(2,1)S(1)}, bf16[256,512]{1,0:T(8,128)(2,1)}, u32[]{:S(2)}, u32[]{:S(2)}) collective-permute-start(bf16[256,512]{1,0:T(8,128)(2,1)S(1)} %bitcast.239), channel_id=1, source_target_pairs={{0,3},{1,4},{2,5},{3,6},{4,7},{5,8},{6,9},{7,10},{8,11},{9,12},{10... | collective-permute-start | bytes 786440 | tf_op jit(solution)/shard_map/ppermute | solution.py:15
  67.0 19.4 %copy-start.1 = (bf16[4,256,5,128]{1,3,2,0:T(8,128)(2,1)S(1)}, bf16[4,256,5,128]{1,3,2,0:T(8,128)(2,1)}, u32[]{:S(2)}) copy-start(bf16[4,256,5,128]{1,3,2,0:T(8,128)(2,1)} %fusion.35) | copy-start | bytes 3932164
  107.1 1.2 copy-start.5
  154.4 3.7 %copy-start.3 = (f32[4,1024,128]{2,1,0:T(8,128)S(1)}, f32[4,1024,128]{2,1,0:T(8,128)}, u32[]{:S(2)}) copy-start(f32[4,1024,128]{2,1,0:T(8,128)} %get-tuple-element.63) | copy-start | bytes 6291460
  158.4 11.8 %copy-start.4 = (f32[4,1024,128]{2,1,0:T(8,128)S(1)}, f32[4,1024,128]{2,1,0:T(8,128)}, u32[]{:S(2)}) copy-start(f32[4,1024,128]{2,1,0:T(8,128)} %get-tuple-element.62) | copy-start | bytes 6291460
  158.7 39.7 %collective-permute-start.11 = (f32[4,256,128]{2,0,1:T(4,128)S(1)}, f32[4,256,128]{2,0,1:T(4,128)S(1)}, u32[]{:S(2)}, u32[]{:S(2)}) collective-permute-start(f32[4,256,128]{2,0,1:T(4,128)S(1)} %bitcast.236), channel_id=1, source_target_pairs={{3,0},{4,1},{5,2},{6,3},{7,4},{8,5},{9,6},{10,7},{11,8},{12,9},{13... | collective-permute-start | bytes 1572872 | tf_op jit(solution)/shard_map/ppermute | solution.py:15
  166.0 43.8 %collective-permute-start.9 = (f32[4,256,128]{2,0,1:T(4,128)}, f32[4,256,128]{2,0,1:T(4,128)}, u32[]{:S(2)}, u32[]{:S(2)}) collective-permute-start(f32[4,256,128]{2,0,1:T(4,128)} %bitcast.170), channel_id=1, source_target_pairs={{1,0},{2,1},{3,2},{4,3},{5,4},{6,5},{7,6},{8,7},{9,8},{10,9},{11,1... | collective-permute-start | bytes 1572872 | tf_op jit(solution)/shard_map/ppermute | solution.py:15
  168.0 51.1 %collective-permute-start.10 = (f32[4,256,128]{2,0,1:T(4,128)}, f32[4,256,128]{2,0,1:T(4,128)}, u32[]{:S(2)}, u32[]{:S(2)}) collective-permute-start(f32[4,256,128]{2,0,1:T(4,128)} %bitcast.169), channel_id=1, source_target_pairs={{2,0},{3,1},{4,2},{5,3},{6,4},{7,5},{8,6},{9,7},{10,8},{11,9},{12,... | collective-permute-start | bytes 1572872 | tf_op jit(solution)/shard_map/ppermute | solution.py:15
  170.3 30.0 %copy-start.2 = (f32[4,256,5,128]{1,3,2,0:T(8,128)S(1)}, f32[4,256,5,128]{1,3,2,0:T(8,128)}, u32[]{:S(2)}) copy-start(f32[4,256,5,128]{1,3,2,0:T(8,128)} %get-tuple-element.61) | copy-start | bytes 7864324
  170.4 30.0 %copy-start.9 = (f32[2560]{0:T(1024)S(1)}, f32[2560]{0:T(1024)}, u32[]{:S(2)}) copy-start(f32[2560]{0:T(1024)} %param.12) | copy-start | bytes 30724
  173.0 93.9 %collective-permute-start.8 = (f32[4,256,128]{2,0,1:T(4,128)}, f32[4,256,128]{2,0,1:T(4,128)}, u32[]{:S(2)}, u32[]{:S(2)}) collective-permute-start(f32[4,256,128]{2,0,1:T(4,128)} %bitcast.171), channel_id=1, source_target_pairs={{3,0},{4,1},{5,2},{6,3},{7,4},{8,5},{9,6},{10,7},{11,8},{12,9},{13... | collective-permute-start | bytes 1572872 | tf_op jit(solution)/shard_map/ppermute | solution.py:15
  174.9 103.2 %collective-permute-start.6 = (f32[4,256,128]{2,0,1:T(4,128)}, f32[4,256,128]{2,0,1:T(4,128)}, u32[]{:S(2)}, u32[]{:S(2)}) collective-permute-start(f32[4,256,128]{2,0,1:T(4,128)} %bitcast.173), channel_id=1, source_target_pairs={{1,0},{2,1},{3,2},{4,3},{5,4},{6,5},{7,6},{8,7},{9,8},{10,9},{11,1... | collective-permute-start | bytes 1572872 | tf_op jit(solution)/shard_map/ppermute | solution.py:15
  198.4 2.4 copy-start.6
  198.4 87.7 %collective-permute-start.7 = (f32[4,256,128]{2,0,1:T(4,128)S(1)}, f32[4,256,128]{2,0,1:T(4,128)}, u32[]{:S(2)}, u32[]{:S(2)}) collective-permute-start(f32[4,256,128]{2,0,1:T(4,128)S(1)} %bitcast.235), channel_id=1, source_target_pairs={{2,0},{3,1},{4,2},{5,3},{6,4},{7,5},{8,6},{9,7},{10,8},{11,9},{12,... | collective-permute-start | bytes 1572872 | tf_op jit(solution)/shard_map/ppermute | solution.py:15
  (3 other events, 3.7 us)
Sparse Core Ops, SparseCore 0:
  158.3 162.5 all-gather.2
